TPU v7x, 32 devices: a whole 2x2x4 slice. The times are simulated.
32 devices in a mesh: range: 8 (over y, x, core), pulse: 4 (over z).
Axes of the slice: x: 2, y: 2, z: 4, core: 2. Of those that a mesh axis runs over, the one named last changes fastest.
Arguments:
- samples: float32 [8192, 2048], P('range', 'pulse'), may hold values from -100 to 100
- taps: float32 [128], replicated, may hold values from -0.5 to 0.5
- taper: float32 [64], P('pulse'), may hold values from 0.5 to 1.5
Outputs:
- whitened: float32 [8192, 2048], P('range', 'pulse')
All inputs are finite; a program needn't handle non-finite values.
Results may differ from a plain program's by a relative error of at most 0.0003.
Values sent between devices are 32-bit elements; how exact they have to be, the bound alone decides.
A program may use at most 64 MiB of HBM per device.

v0:
```python
import math

import jax
import jax.numpy as jnp
from jax import lax
from jax.sharding import PartitionSpec as P

LOADING = 0.05


def padded_2(block, sides, width):
    for axis, dim in sides:
        count = lax.axis_size(axis)
        forward = [(i, i + 1) for i in range(count - 1)]
        backward = [(target, source) for source, target in forward]
        low = lax.ppermute(
            lax.slice_in_dim(block, block.shape[dim] - width, None, axis=dim), axis, forward
        )
        high = lax.ppermute(lax.slice_in_dim(block, 0, width, axis=dim), axis, backward)
        block = jnp.concatenate([low, block, high], axis=dim)
    return block


def toeplitz(taps, tile_rows):
    tap_count = taps.shape[0]
    padded_taps = jnp.concatenate([taps, jnp.zeros((tile_rows,), taps.dtype)])
    repeated = jnp.tile(padded_taps, tile_rows)[: tile_rows * (tap_count + tile_rows - 1)]
    return repeated.reshape(tile_rows, tap_count + tile_rows - 1)


def doppler_matrix(pulses):
    position = jnp.arange(pulses, dtype=jnp.int32)
    phase_index = position[:, None] * position[None, :] % pulses
    angles = phase_index.astype(jnp.float32) * (2.0 * math.pi / pulses)
    amplitude = 1.0 / math.sqrt(pulses)
    cosine = jnp.cos(angles) * amplitude
    sine_part = jnp.sin(angles) * amplitude
    real_in = jnp.stack([cosine, -sine_part], axis=1)
    imag_in = jnp.stack([sine_part, cosine], axis=1)
    return jnp.stack([real_in, imag_in], axis=1)


def transform(received, doppler_table, pulses, group_width):
    part_rows = received.shape[0]
    arranged = received.reshape(part_rows, pulses, group_width // 2, 2)
    spectrum = jnp.einsum(
        "rpca,pabk->rkcb", arranged, doppler_table, precision=lax.Precision.HIGHEST
    )
    return spectrum.reshape(part_rows, pulses, group_width)


def local(samples, taps, taper):
    gate_rows, columns = samples.shape
    tap_count = taps.shape[0]
    half_taps = tap_count // 2
    bin_count = taper.shape[0]
    pulse_devices = lax.axis_size("pulse")
    range_devices = lax.axis_size("range")
    pulses = bin_count * pulse_devices
    channels = columns // (2 * bin_count)
    padded = padded_2(samples, (("range", 0),), half_taps)
    tile_rows = min(128, gate_rows)
    matrix = toeplitz(taps, tile_rows)

    def compress_block(first_row):
        window = lax.dynamic_slice_in_dim(padded, first_row, tile_rows + tap_count - 1, 0)
        return jnp.dot(
            matrix, window, precision=lax.Precision.HIGHEST, preferred_element_type=jnp.float32
        )

    starts = jnp.arange(gate_rows // tile_rows, dtype=jnp.int32) * tile_rows
    compressed = lax.map(compress_block, starts).reshape(gate_rows, columns)
    tapered = compressed * jnp.repeat(taper, 2 * channels)[None, :]
    doppler_table = doppler_matrix(pulses)
    gathered = lax.all_to_all(tapered, "pulse", split_axis=0, concat_axis=1, tiled=True)
    spectrum = transform(gathered, doppler_table, pulses, 2 * channels).reshape(
        gathered.shape[0], pulses * 2 * channels
    )
    doppler = lax.all_to_all(spectrum, "pulse", split_axis=1, concat_axis=0, tiled=True)
    total_gates = gate_rows * range_devices
    identity = jnp.eye(columns, dtype=jnp.float32)
    local_gram = lax.dot_general(
        doppler, doppler, (((0,), (0,)), ((), ())), precision=lax.Precision.HIGHEST
    )
    summed = lax.psum(local_gram, "range")
    factor = jnp.linalg.cholesky(summed / total_gates + LOADING * identity)
    return lax.linalg.triangular_solve(
        factor, doppler, left_side=False, lower=True, transpose_a=True
    )


def solution(mesh):
    placed = (P("range", "pulse"), P(), P("pulse"))
    return jax.shard_map(
        local, mesh=mesh, in_specs=placed, out_specs=P("range", "pulse"), check_vma=False
    )
```

profile of v0, /device:TPU:0, one launch (start us, length us, event | category | flops | bytes accessed | tf_op | source)
XLA Modules:
  0.0 417.9 jit_solution(12553008292331072088)
XLA Ops:
  7.5 2.4 collective-permute-start
  9.9 1.3 collective-permute-start.1
  13.1 2.1 collective-permute-done.1
  15.3 1.8 pad_maximum_fusion
  17.1 36.9 %while.11 = (s32[]{:T(128)}, f32[8,128,512]{2,1,0:T(8,128)}, s32[8]{0:T(128)S(1)}, f32[1152,512]{1,0:T(8,128)S(1)}, f32[128,255]{1,0:T(8,128)S(1)}, /*index=5*/s32[]{:T(128)}, s32[]{:T(128)}, s32[]{:T(128)}) while((s32[]{:T(128)}, f32[8,128,512]{2,1,0:T(8,128)}, s32[8]{0:T(128)S(1)}, f32[1152,512]{1,0:T(8,128)S(1)}, f32[128,255]{1,0:T(8,128)S(1)}, ...), condition=%wide.region_1.2_spmd, body=%wide.region_0.1_spmd.sunk | while | flops 200540160 | bytes 1966727 | solution.py:72
  19.8 1.0 convolution_bitcast_fusion.2
  29.0 1.0 convolution_bitcast_fusion.2
  33.6 1.0 convolution_bitcast_fusion.2
  38.3 1.0 convolution_bitcast_fusion.2
  42.9 1.0 convolution_bitcast_fusion.2
  53.9 3.2 bitcast_multiply_fusion
  57.1 4.9 %all-to-all-start = ((f32[4,256,512]{2,1,0:T(8,128)}), f32[4,256,512]{2,1,0:T(8,128)S(1)}, u32[]{:S(2)}, u32[]{:S(2)}) async-start(f32[4,256,512]{2,1,0:T(8,128)} %bitcast_multiply_fusion), calls=%async_computation | async-start | bytes 4194304 | tf_op jit(solution)/shard_map/all_to_all | solution.py:75
  62.3 48.3 %all-to-all-done = f32[4,256,512]{2,1,0:T(8,128)S(1)} async-done(((f32[4,256,512]{2,1,0:T(8,128)}), f32[4,256,512]{2,1,0:T(8,128)S(1)}, u32[]{:S(2)}, u32[]{:S(2)}) %all-to-all-start) | async-done | bytes 2097184 | tf_op jit(solution)/shard_map/all_to_all | solution.py:75
  110.6 1.8 copy.19
  112.4 2.5 reshape.143
  114.9 3.0 fusion.7
  117.9 1.6 copy.21
  119.5 2.4 all_to_all.26
  122.0 2.9 copy.22
  124.9 53.1 %all_to_all.32 = f32[256,4,512]{2,0,1:T(8,128)S(1)} all-to-all(f32[256,4,512]{2,0,1:T(8,128)} %copy.22), channel_id=1, replica_groups=mesh['range'=8,'pulse'=4] {'pulse'}, dimensions={1} | all-to-all | bytes 4194304 | tf_op jit(solution)/shard_map/all_to_all | solution.py:79
  178.0 4.5 %fusion.16 = f32[512,512]{0,1:T(8,128)} fusion(f32[256,4,512]{2,0,1:T(8,128)S(1)} %all_to_all.32), kind=kOutput, calls=%fused_computation.21 | convolution fusion | flops 3221225472 | bytes 3145728 | tf_op jit(solution)/shard_map/dot_general | solution.py:82
  182.6 57.3 %all-reduce.4.cloned.1.call-done = f32[512,512]{0,1:T(8,128)} async-done(((f32[512,512]{0,1:T(8,128)}), f32[512,512]{0,1:T(8,128)}) %all-reduce.4.cloned.1.call-update) | async-done | bytes 1048592 | tf_op jit(solution)/shard_map/psum | solution.py:85
  239.8 2.4 select_add_fusion
  242.2 2.6 copy.25
  244.8 1.5 fusion.25
  247.3 11.7 %cholesky.103 = f32[128,128]{1,0:T(8,128)S(1)} custom-call(f32[128,128]{1,0:T(8,128)S(1)} %cholesky.263), custom_call_target="Cholesky" | custom-call | tf_op jit(solution)/shard_map/jit(cholesky)/cholesky | solution.py:86
  259.0 9.8 %custom-call.30 = f32[1,128,128]{1,2,0:T(8,128)S(1)} custom-call(f32[1,128,128]{2,1,0:T(8,128)S(1)} %get-tuple-element.76), custom_call_target="InvertDiagBlocksLowerTriangular" | custom-call | tf_op jit(solution)/shard_map/jit(cholesky)/cholesky | solution.py:86
  268.8 1.2 fusion.31
  270.1 1.3 convolution_subtract_fusion.2
  271.4 11.9 %cholesky.215 = f32[128,128]{1,0:T(8,128)S(1)} custom-call(f32[128,128]{1,0:T(8,128)S(1)} %cholesky.267), custom_call_target="Cholesky" | custom-call | tf_op jit(solution)/shard_map/jit(cholesky)/cholesky | solution.py:86
  286.4 11.3 %custom-call.31 = f32[1,128,128]{1,2,0:T(8,128)} custom-call(f32[1,128,128]{2,1,0:T(8,128)} %get-tuple-element.74), custom_call_target="InvertDiagBlocksLowerTriangular" | custom-call | tf_op jit(solution)/shard_map/jit(cholesky)/cholesky | solution.py:86
  298.5 1.2 convolution_dynamic-update-slice_fusion
  299.7 1.5 convolution_subtract_fusion.3
  301.2 11.7 %cholesky.236 = f32[128,128]{1,0:T(8,128)S(1)} custom-call(f32[128,128]{1,0:T(8,128)S(1)} %cholesky.272), custom_call_target="Cholesky" | custom-call | tf_op jit(solution)/shard_map/jit(cholesky)/cholesky | solution.py:86
  313.1 9.8 %custom-call.32 = f32[1,128,128]{1,2,0:T(8,128)S(1)} custom-call(f32[1,128,128]{2,1,0:T(8,128)S(1)} %get-tuple-element.72), custom_call_target="InvertDiagBlocksLowerTriangular" | custom-call | tf_op jit(solution)/shard_map/jit(cholesky)/cholesky | solution.py:86
  323.4 1.3 convolution_subtract_fusion.4
  324.7 11.7 %cholesky.253 = f32[128,128]{1,0:T(8,128)S(1)} custom-call(f32[128,128]{1,0:T(8,128)S(1)} %convolution_subtract_fusion.4), custom_call_target="Cholesky" | custom-call | tf_op jit(solution)/shard_map/jit(cholesky)/cholesky | solution.py:86
  341.8 1.1 select_select_fusion
  342.9 14.5 %while.12 = (s32[]{:T(128)}, f32[512,512]{0,1:T(8,128)}, s32[4,2]{0,1:T(2,128)S(1)}, f32[4,128,128]{2,1,0:T(8,128)}, s32[]{:T(128)}) while((s32[]{:T(128)}, f32[512,512]{0,1:T(8,128)}, s32[4,2]{0,1:T(2,128)S(1)}, f32[4,128,128]{2,1,0:T(8,128)}, s32[]{:T(128)}) %tuple.43), condition=%wide.while_cond, body=%wide.while_body.sunk | while | flops 2 | bytes 393829 | solution.py:87
  343.6 2.2 dynamic-slice.7
  347.2 2.2 dynamic-slice.7
  350.9 2.2 dynamic-slice.7
  354.5 2.2 dynamic-slice.7
  357.4 40.4 %custom-call.33 = f32[4,128,128]{1,2,0:T(8,128)S(1)} custom-call(f32[4,128,128]{2,1,0:T(8,128)} %get-tuple-element.40), custom_call_target="InvertDiagBlocksLowerTriangular" | custom-call | tf_op jit(solution)/shard_map/triangular_solve | solution.py:87
  398.4 1.8 convolution_subtract_fusion.1
  400.9 2.8 convolution_subtract_fusion
  404.3 3.7 fusion.19
  408.8 1.8 copy.34
  (92 shorter events, 35.0 us)
Async XLA Ops:
  7.5 5.6 %collective-permute-start = (f32[64,512]{1,0:T(8,128)S(1)}, f32[64,512]{1,0:T(8,128)S(1)}, u32[]{:S(2)}, u32[]{:S(2)}) collective-permute-start(f32[64,512]{1,0:T(8,128)S(1)} %get-tuple-element.69), channel_id=1, source_target_pairs={{0,4},{4,8},{8,12},{12,16},{16,20},{20,24},{24,28},{1,5},{5,9},{9,... | collective-permute-start | bytes 393224 | tf_op jit(solution)/shard_map/ppermute | solution.py:16
  9.9 5.3 %collective-permute-start.1 = (f32[64,512]{1,0:T(8,128)S(1)}, f32[64,512]{1,0:T(8,128)S(1)}, u32[]{:S(2)}, u32[]{:S(2)}) collective-permute-start(f32[64,512]{1,0:T(8,128)S(1)} %get-tuple-element.70), channel_id=1, source_target_pairs={{4,0},{8,4},{12,8},{16,12},{20,16},{24,20},{28,24},{5,1},{9,5},{13... | collective-permute-start | bytes 393224 | tf_op jit(solution)/shard_map/ppermute | solution.py:19
  57.1 53.5 %all-to-all-start = ((f32[4,256,512]{2,1,0:T(8,128)}), f32[4,256,512]{2,1,0:T(8,128)S(1)}, u32[]{:S(2)}, u32[]{:S(2)}) async-start(f32[4,256,512]{2,1,0:T(8,128)} %bitcast_multiply_fusion), calls=%async_computation | async-start | bytes 4194304 | tf_op jit(solution)/shard_map/all_to_all | solution.py:75
  62.0 177.8 %all-reduce.4.cloned.1.call-start = ((), (), s32[]{:S(2)}) async-start(), calls=%async_computation.2 | async-start | bytes 2097152 | tf_op jit(solution)/shard_map/psum | solution.py:85
  239.8 5.0 %copy-start = (f32[512,512]{0,1:T(8,128)S(1)}, f32[512,512]{0,1:T(8,128)}, u32[]{:S(2)}) copy-start(f32[512,512]{0,1:T(8,128)} %all-reduce.4.cloned.1.call-done) | copy-start | bytes 3145732
  246.3 1.0 copy-start.1
Sparse Core Ops, SparseCore 0:
  182.7 57.1 all-reduce.3
where the time goes:
time: 426 us; the launch traced here: 418 us
  other arithmetic  132 us (31%)
  waiting for transfers between devices  108 us (25%)
  blocking collectives  53.1 us (12%)
  local copies, waits for them, and re-layouts  49.8 us (12%)
  matrix products  33.3 us (8%)
  loops' own time  16.8 us (4%)
  between operations  16.7 us (4%)
  starting transfers between devices  8.57 us (2%)
    another operation x15, other arithmetic, local(): factor = jnp.linalg.cholesky(summed / total_gates + LOADING * identity)  81.3 us
    psum x1, waiting for transfers between devices, local(): summed = lax.psum(local_gram, 'range')  57.3 us
    all_to_all x1, blocking collectives, local(): lax.all_to_all(spectrum, 'pulse', split_axis=1, concat_axis=0, tiled=True)  53.1 us
    all_to_all x1, waiting for transfers between devices, local(): lax.all_to_all(tapered, 'pulse', split_axis=0, concat_axis=1, tiled=True)  48.3 us
    another operation x4, other arithmetic, local(): lax.linalg.triangular_solve(factor, doppler, left_side=False, lower=True,...  41.6 us
    another operation x1, loops' own time, local(): compressed = lax.map(compress_block, starts).reshape(gate_rows, columns)  16.7 us
    another operation x20, local copies, waits for them, and re-layouts  14.5 us
    another operation x7, matrix products, local(): lax.linalg.triangular_solve(factor, doppler, left_side=False, lower=True,...  10.8 us
  transfers between devices with their start and end apart: 4, of which 3 were waited for; matrix products, arithmetic and copies ran while one was open for 1% of the time, Pallas kernels for 0%

commit v1 on v0

--- a/solution.py
+++ b/solution.py
@@ -1,8 +1,11 @@
+import functools
 import math
 
 import jax
 import jax.numpy as jnp
 from jax import lax
+from jax.experimental import pallas as pl
+from jax.experimental.pallas import tpu as pltpu
 from jax.sharding import PartitionSpec as P
 
 LOADING = 0.05
@@ -47,6 +50,107 @@
         "rpca,pabk->rkcb", arranged, doppler_table, precision=lax.Precision.HIGHEST
     )
     return spectrum.reshape(part_rows, pulses, group_width)
+
+
+BLOCK = 128
+PANEL = 16
+HIGHEST = lax.Precision.HIGHEST
+
+
+def split3(x):
+    high = x.astype(jnp.bfloat16)
+    rest = x - high.astype(jnp.float32)
+    middle = rest.astype(jnp.bfloat16)
+    low = (rest - middle.astype(jnp.float32)).astype(jnp.bfloat16)
+    return high, middle, low
+
+
+def eliminate_panel(work_ref, first, block):
+    last = first + PANEL
+    tile = work_ref[first:last, :]
+    width = tile.shape[1]
+    row = lax.broadcasted_iota(jnp.int32, (PANEL, block), 0)
+    columns = [
+        jnp.broadcast_to(tile[:, first + c : first + c + 1], (PANEL, block)) for c in range(PANEL)
+    ]
+    left, right = tile[:, :block], tile[:, block:]
+    for r in range(PANEL):
+        inverse = lax.rsqrt(columns[r][r : r + 1, :])
+        below = jnp.where(row > r, columns[r] * inverse, 0.0)
+        for c in range(r + 1, PANEL):
+            columns[c] = columns[c] - below * (columns[c][r : r + 1, :] * inverse)
+        left_row = left[r : r + 1, :] * inverse
+        right_row = right[r : r + 1, :] * inverse
+        left = jnp.where(row == r, left_row, left - below * left_row)
+        right = jnp.where(row == r, right_row, right - below * right_row)
+    tile = jnp.concatenate([left, right], axis=1)
+    work_ref[first:last, :] = tile
+    if last < block:
+        high, middle, low = split3(tile)
+        lhs = jnp.concatenate([high, high, middle, middle, high, low], axis=0)[:, :block]
+        rhs = jnp.concatenate([high, middle, high, middle, low, high], axis=0)
+        update = lax.dot_general(
+            lhs, rhs, (((0,), (0,)), ((), ())), preferred_element_type=jnp.float32
+        )
+        work_ref[last:, :] = work_ref[last:, :] - update[last:, :]
+
+
+def whiten_kernel(total_gates, gram_ref, snapshot_ref, out_ref, cov_ref, work_ref):
+    size = gram_ref.shape[0]
+    block = min(BLOCK, size)
+    rows = lax.broadcasted_iota(jnp.int32, (size, size), 0)
+    cols = lax.broadcasted_iota(jnp.int32, (size, size), 1)
+    cov_ref[...] = gram_ref[...] * (1.0 / total_gates) + jnp.where(rows == cols, LOADING, 0.0)
+    out_ref[...] = snapshot_ref[...]
+    transposed = (((1,), (1,)), ((), ()))
+
+    def step(index, carry):
+        start = pl.multiple_of(index * block, block)
+        here = pl.ds(start, block)
+        r = lax.broadcasted_iota(jnp.int32, (block, block), 0)
+        c = lax.broadcasted_iota(jnp.int32, (block, block), 1)
+        work_ref[:, :block] = cov_ref[here, here]
+        work_ref[:, block:] = jnp.where(r == c, 1.0, 0.0)
+        for first in range(0, block, PANEL):
+            eliminate_panel(work_ref, first, block)
+        inverse = work_ref[:, block:]
+        panel = lax.dot_general(
+            cov_ref[:, here], inverse, transposed, precision=HIGHEST,
+            preferred_element_type=jnp.float32,
+        )
+        below = lax.broadcasted_iota(jnp.int32, (size, block), 0) >= start + block
+        panel = jnp.where(below, panel, 0.0)
+        cov_ref[...] = cov_ref[...] - lax.dot_general(
+            panel, panel, transposed, precision=HIGHEST, preferred_element_type=jnp.float32
+        )
+        solved = lax.dot_general(
+            out_ref[:, here], inverse, transposed, precision=HIGHEST,
+            preferred_element_type=jnp.float32,
+        )
+        out_ref[...] = out_ref[...] - lax.dot_general(
+            solved, panel, transposed, precision=HIGHEST, preferred_element_type=jnp.float32
+        )
+        out_ref[:, here] = solved
+        return carry
+
+    lax.fori_loop(0, size // block, step, 0)
+
+
+def whiten(gram, snapshot, total_gates):
+    size = gram.shape[0]
+    block = min(BLOCK, size)
+    return pl.pallas_call(
+        functools.partial(whiten_kernel, total_gates),
+        out_shape=jax.ShapeDtypeStruct(snapshot.shape, jnp.float32),
+        in_specs=[pl.BlockSpec(memory_space=pltpu.VMEM)] * 2,
+        out_specs=pl.BlockSpec(memory_space=pltpu.VMEM),
+        scratch_shapes=[
+            pltpu.VMEM((size, size), jnp.float32),
+            pltpu.VMEM((block, 2 * block), jnp.float32),
+        ],
+        compiler_params=pltpu.CompilerParams(vmem_limit_bytes=32 << 20),
+        name="whiten",
+    )(gram, snapshot)
 
 
 def local(samples, taps, taper):
@@ -62,14 +166,18 @@
     tile_rows = min(128, gate_rows)
     matrix = toeplitz(taps, tile_rows)
 
-    def compress_block(first_row):
-        window = lax.dynamic_slice_in_dim(padded, first_row, tile_rows + tap_count - 1, 0)
-        return jnp.dot(
-            matrix, window, precision=lax.Precision.HIGHEST, preferred_element_type=jnp.float32
-        )
-
-    starts = jnp.arange(gate_rows // tile_rows, dtype=jnp.int32) * tile_rows
-    compressed = lax.map(compress_block, starts).reshape(gate_rows, columns)
+    band = jnp.concatenate([matrix, jnp.zeros((tile_rows, 1), matrix.dtype)], axis=1)
+    tiles = padded.reshape(-1, tile_rows, columns)
+    span = gate_rows // tile_rows
+    compressed = 0.0
+    for part in range(band.shape[1] // tile_rows):
+        compressed = compressed + jnp.einsum(
+            "ab,ibj->iaj",
+            band[:, part * tile_rows : (part + 1) * tile_rows],
+            tiles[part : part + span],
+            precision=HIGHEST,
+        )
+    compressed = compressed.reshape(gate_rows, columns)
     tapered = compressed * jnp.repeat(taper, 2 * channels)[None, :]
     doppler_table = doppler_matrix(pulses)
     gathered = lax.all_to_all(tapered, "pulse", split_axis=0, concat_axis=1, tiled=True)
@@ -78,15 +186,11 @@
     )
     doppler = lax.all_to_all(spectrum, "pulse", split_axis=1, concat_axis=0, tiled=True)
     total_gates = gate_rows * range_devices
-    identity = jnp.eye(columns, dtype=jnp.float32)
     local_gram = lax.dot_general(
         doppler, doppler, (((0,), (0,)), ((), ())), precision=lax.Precision.HIGHEST
     )
     summed = lax.psum(local_gram, "range")
-    factor = jnp.linalg.cholesky(summed / total_gates + LOADING * identity)
-    return lax.linalg.triangular_solve(
-        factor, doppler, left_side=False, lower=True, transpose_a=True
-    )
+    return whiten(summed, doppler, total_gates)
 
 
 def solution(mesh):

time: 426 us -> 249 us (0.58); the launches traced: 418 us -> 249 us
  other arithmetic: 132 us -> 6.05 us
  local copies, waits for them, and re-layouts: 49.8 us -> 15.1 us
  Pallas kernels: 0 us -> 31.4 us
  matrix products: 33.3 us -> 13.4 us
  loops' own time: 16.8 us -> 0 us
    another operation x19 -> x0, other arithmetic: 123 us -> none  [the longest x15 81.3 us: local(): factor = jnp.linalg.cholesky(summed / total_gates + LOADING * identity)]
    pallas_call x0 -> x1, Pallas kernels: none -> 31.4 us  [whiten(): pl.pallas_call(functools.partial(whiten_kernel, total_gates), out_shape=j...]
    another operation x35 -> x0, local copies, waits for them, and re-layouts: 19.9 us -> none
    another operation x13 -> x0, matrix products: 17.8 us -> none  [the longest x7 10.8 us: local(): lax.linalg.triangular_solve(factor, doppler, left_side=False, lower=True,...]
    another operation x2 -> x0, loops' own time: 16.8 us -> none  [the longest x1 16.7 us: local(): compressed = lax.map(compress_block, starts).reshape(gate_rows, columns)]
    dynamic_update_slice x16 -> x0, local copies, waits for them, and re-layouts: 6.83 us -> none  [local(): compressed = lax.map(compress_block, starts).reshape(gate_rows, columns)]
    dynamic_slice x8 -> x0, local copies, waits for them, and re-layouts: 5.3 us -> none  [local(): compressed = lax.map(compress_block, starts).reshape(gate_rows, columns)]
where the time goes in v1:
time: 249 us
  waiting for transfers between devices  108 us (43%)
  blocking collectives  53.1 us (21%)
  Pallas kernels  31.4 us (13%)
  local copies, waits for them, and re-layouts  15.1 us (6%)
  between operations  13.5 us (5%)
  matrix products  13.4 us (5%)
  starting transfers between devices  8.58 us (3%)
  other arithmetic  6.05 us (2%)
    psum x1, waiting for transfers between devices, local(): summed = lax.psum(local_gram, 'range')  57.3 us
    all_to_all x1, blocking collectives, local(): lax.all_to_all(spectrum, 'pulse', split_axis=1, concat_axis=0, tiled=True)  53.1 us
    all_to_all x1, waiting for transfers between devices, local(): lax.all_to_all(tapered, 'pulse', split_axis=0, concat_axis=1, tiled=True)  48.3 us
    pallas_call x1, Pallas kernels, whiten(): pl.pallas_call(functools.partial(whiten_kernel, total_gates), out_shape=j...  31.4 us
    all_to_all x2, local copies, waits for them, and re-layouts, local(): lax.all_to_all(spectrum, 'pulse', split_axis=1, concat_axis=0, tiled=True)  5.37 us
  transfers between devices with their start and end apart: 4, of which 3 were waited for; matrix products, arithmetic and copies ran while one was open for 1% of the time, Pallas kernels for 0%

profile of v1, /device:TPU:0, one launch (start us, length us, event | category | flops | bytes accessed | tf_op | source)
XLA Modules:
  0.0 248.8 jit_solution(5949620204152449024)
XLA Ops:
  6.5 1.0 fusion.25
  7.5 2.4 collective-permute-start
  9.9 1.3 collective-permute-start.1
  11.2 0.7 concatenate.14
  11.9 0.1 copy.15
  12.0 0.3 reshape.109
  12.3 0.7 broadcast_in_dim.2
  13.1 0.1 mul.119
  13.1 0.0 collective-permute-done
  13.1 2.1 collective-permute-done.1
  15.3 2.6 %pad_maximum_fusion.1 = (f32[1024,512]{1,0:T(8,128)S(1)}, f32[1024,512]{1,0:T(8,128)S(1)}) fusion(f32[1024,512]{1,0:T(8,128)} %param.3, f32[64,512]{1,0:T(8,128)S(1)} %collective-permute-done, f32[64,512]{1,0:T(8,128)S(1)} %collective-permute-done.1), kind=kLoop, calls=%fused_computation.1 | loop fusion | flops 1048576 | bytes 6553600 | tf_op jit(solution)/shard_map/concatenate | solution.py:23
  17.9 2.1 fusion.14
  20.0 2.3 convolution_add_fusion
  22.3 1.8 copy.7
  24.1 3.1 %broadcast_multiply_fusion = f32[4,256,512]{1,2,0:T(8,128)} fusion(f32[4,256,512]{1,2,0:T(8,128)} %copy.7, f32[512]{0:T(512)S(1)} %mul.119), kind=kLoop, calls=%fused_computation.10 | loop fusion | flops 524288 | bytes 4196352 | tf_op jit(solution)/shard_map/mul | solution.py:181
  27.2 4.9 %all-to-all-start = ((f32[4,256,512]{1,2,0:T(8,128)}), f32[4,256,512]{1,2,0:T(8,128)S(1)}, u32[]{:S(2)}, u32[]{:S(2)}) async-start(f32[4,256,512]{1,2,0:T(8,128)} %broadcast_multiply_fusion), calls=%async_computation | async-start | bytes 4194304 | tf_op jit(solution)/shard_map/all_to_all | solution.py:183
  32.1 0.0 all-reduce.4.cloned.1.call-start
  32.1 0.1 fusion.22
  32.2 0.2 sine_multiply_fusion
  32.4 48.3 %all-to-all-done = f32[4,256,512]{1,2,0:T(8,128)S(1)} async-done(((f32[4,256,512]{1,2,0:T(8,128)}), f32[4,256,512]{1,2,0:T(8,128)S(1)}, u32[]{:S(2)}, u32[]{:S(2)}) %all-to-all-start) | async-done | bytes 2097184 | tf_op jit(solution)/shard_map/all_to_all | solution.py:183
  80.7 2.2 reshape.111
  82.9 4.5 %fusion.5 = f32[256,64,16,2]{0,1,2,3:T(8,128)S(1)} fusion(f32[256,64,16,2]{0,3,2,1:T(2,128)} %reshape.111, f32[64,1,2,64]{0,3,1,2:T(8,128)S(1)} %get-tuple-element.10, f32[64,1,2,64]{0,3,1,2:T(8,128)S(1)} %get-tuple-element.9), kind=kOutput, calls=%fused_computation.7 | convolution fusion | flops 805322752 | bytes 4259840 | tf_op jit(solution)/shard_map/rpca,pabk->rkcb/dot_general | solution.py:49
  87.5 1.6 copy.9
  89.1 2.4 all_to_all.26
  91.5 2.9 %copy.10 = f32[256,4,512]{2,0,1:T(8,128)} copy(f32[256,4,512]{0,2,1:T(8,128)} %all_to_all.26) | data formatting | bytes 4194304 | tf_op jit(solution)/shard_map/all_to_all | solution.py:187
  94.5 53.1 %all_to_all.32 = f32[256,4,512]{2,0,1:T(8,128)S(1)} all-to-all(f32[256,4,512]{2,0,1:T(8,128)} %copy.10), channel_id=1, replica_groups=mesh['range'=8,'pulse'=4] {'pulse'}, dimensions={1} | all-to-all | bytes 4194304 | tf_op jit(solution)/shard_map/all_to_all | solution.py:187
  147.6 4.5 %fusion.8 = f32[512,512]{1,0:T(8,128)} fusion(f32[256,4,512]{2,0,1:T(8,128)S(1)} %all_to_all.32), kind=kOutput, calls=%fused_computation.9 | convolution fusion | flops 3221225472 | bytes 3145728 | tf_op jit(solution)/shard_map/dot_general | solution.py:189
  152.1 0.0 all-reduce.4.cloned.1.call-update
  152.1 57.3 %all-reduce.4.cloned.1.call-done.gram_ref = f32[512,512]{1,0:T(8,128)} async-done(((f32[512,512]{1,0:T(8,128)}), f32[512,512]{1,0:T(8,128)}) %all-reduce.4.cloned.1.call-update) | async-done | bytes 1048592 | tf_op jit(solution)/shard_map/psum | solution.py:192
  209.4 0.0 copy-start
  209.4 1.2 copy-done
  210.6 31.4 %whiten.1 = f32[1024,512]{1,0:T(8,128)} custom-call(f32[512,512]{1,0:T(8,128)S(1)} %copy-done, f32[1024,512]{1,0:T(8,128)S(1)} %bitcast.52), custom_call_target="tpu_custom_call" | custom-call | tf_op jit(solution)/shard_map/whiten/pallas_call | solution.py:142
  (2 shorter events, 0.0 us)
Async XLA Ops:
  7.5 5.6 %collective-permute-start = (f32[64,512]{1,0:T(8,128)S(1)}, f32[64,512]{1,0:T(8,128)S(1)}, u32[]{:S(2)}, u32[]{:S(2)}) collective-permute-start(f32[64,512]{1,0:T(8,128)S(1)} %get-tuple-element.7), channel_id=1, source_target_pairs={{0,4},{4,8},{8,12},{12,16},{16,20},{20,24},{24,28},{1,5},{5,9},{9,... | collective-permute-start | bytes 393224 | tf_op jit(solution)/shard_map/ppermute | solution.py:19
  9.9 5.3 %collective-permute-start.1 = (f32[64,512]{1,0:T(8,128)S(1)}, f32[64,512]{1,0:T(8,128)S(1)}, u32[]{:S(2)}, u32[]{:S(2)}) collective-permute-start(f32[64,512]{1,0:T(8,128)S(1)} %get-tuple-element.8), channel_id=1, source_target_pairs={{4,0},{8,4},{12,8},{16,12},{20,16},{24,20},{28,24},{5,1},{9,5},{13... | collective-permute-start | bytes 393224 | tf_op jit(solution)/shard_map/ppermute | solution.py:22
  27.2 53.5 %all-to-all-start = ((f32[4,256,512]{1,2,0:T(8,128)}), f32[4,256,512]{1,2,0:T(8,128)S(1)}, u32[]{:S(2)}, u32[]{:S(2)}) async-start(f32[4,256,512]{1,2,0:T(8,128)} %broadcast_multiply_fusion), calls=%async_computation | async-start | bytes 4194304 | tf_op jit(solution)/shard_map/all_to_all | solution.py:183
  32.1 177.3 %all-reduce.4.cloned.1.call-start = ((), (), s32[]{:S(2)}) async-start(), calls=%async_computation.2 | async-start | bytes 2097152 | tf_op jit(solution)/shard_map/psum | solution.py:192
  209.4 1.2 copy-start
Sparse Core Ops, SparseCore 0:
  152.2 57.1 all-reduce.3

commit v2 on v1

--- a/solution.py
+++ b/solution.py
@@ -95,62 +95,172 @@
         work_ref[last:, :] = work_ref[last:, :] - update[last:, :]
 
 
-def whiten_kernel(total_gates, gram_ref, snapshot_ref, out_ref, cov_ref, work_ref):
-    size = gram_ref.shape[0]
-    block = min(BLOCK, size)
-    rows = lax.broadcasted_iota(jnp.int32, (size, size), 0)
-    cols = lax.broadcasted_iota(jnp.int32, (size, size), 1)
-    cov_ref[...] = gram_ref[...] * (1.0 / total_gates) + jnp.where(rows == cols, LOADING, 0.0)
-    out_ref[...] = snapshot_ref[...]
+def lower_blocks(size, block):
+    pairs = [(b, c) for b in range(size // block) for c in range(b + 1)]
+    return [(b * block, c * block, n * block) for n, (b, c) in enumerate(pairs)]
+
+
+def sum_over_range(part_ref, pair_ref, half_ref, inbox_ref, total_ref, sems):
+    pair_send, pair_recv, out_send, out_recv, back_send, back_recv, side_send, side_recv = sems
+    me, count = lax.axis_index("range"), lax.axis_size("range")
+    groups = count // 2
+    side, group = lax.rem(me, 2), me // 2
+    sibling = me + 1 - 2 * side
+    half, chunk = half_ref.shape[0], half_ref.shape[0] // groups
+
+    def send(src, dst, send_sem, recv_sem, target):
+        copy = pltpu.make_async_remote_copy(
+            src_ref=src, dst_ref=dst, send_sem=send_sem, recv_sem=recv_sem,
+            device_id={"range": target}, device_id_type=pl.DeviceIdType.MESH,
+        )
+        copy.start()
+        return copy
+
+    def peer(shift):
+        return 2 * lax.rem(group + shift, groups) + side
+
+    def rows(whose, of_group):
+        return pl.ds(pl.multiple_of(whose * half + of_group * chunk, 8), chunk)
+
+    theirs = pl.ds(pl.multiple_of((1 - side) * half, 8), half)
+    mine = pl.ds(pl.multiple_of(side * half, 8), half)
+    first = send(part_ref.at[theirs], pair_ref, pair_send, pair_recv, sibling)
+    first.wait_recv()
+    half_ref[...] = part_ref[mine] + pair_ref[...]
+    outs = []
+    for shift in range(1, groups):
+        to = lax.rem(group + shift, groups)
+        outs.append(
+            send(
+                half_ref.at[rows(0, to)], inbox_ref.at[shift - 1],
+                out_send.at[shift - 1], out_recv.at[shift - 1], peer(shift),
+            )
+        )
+    own = half_ref[rows(0, group)]
+    for shift in range(1, groups):
+        outs[shift - 1].wait_recv()
+        own = own + inbox_ref[shift - 1]
+    total_ref[rows(side, group)] = own
+    source = total_ref.at[rows(side, group)]
+    backs = [
+        send(source, source, back_send.at[s - 1], back_recv.at[s - 1], peer(s))
+        for s in range(1, groups)
+    ]
+    sides = [send(source, source, side_send.at[0], side_recv.at[0], sibling)]
+    for shift in range(1, groups):
+        backs[shift - 1].wait_recv()
+        landed = total_ref.at[rows(side, lax.rem(group + groups - shift, groups))]
+        sides.append(send(landed, landed, side_send.at[shift], side_recv.at[shift], sibling))
+    for copy in sides:
+        copy.wait_recv()
+    for copy in [first] + outs + backs + sides:
+        copy.wait_send()
+
+
+def greet(axis_targets):
+    barrier = pltpu.get_barrier_semaphore()
+    for axis, target in axis_targets:
+        pl.semaphore_signal(
+            barrier, inc=1, device_id={axis: target}, device_id_type=pl.DeviceIdType.MESH
+        )
+    pl.semaphore_wait(barrier, len(axis_targets))
+
+
+def range_partners():
+    me, count = lax.axis_index("range"), lax.axis_size("range")
+    groups, side, group = count // 2, lax.rem(me, 2), me // 2
+    found = [("range", me + 1 - 2 * side)]
+    for shift in range(1, groups):
+        found.append(("range", 2 * lax.rem(group + shift, groups) + side))
+    return found
+
+
+def factor_and_solve(total_gates, total_ref, out_ref, cov_ref, work_ref):
+    size = cov_ref.shape[0]
+    block = work_ref.shape[0]
+    r = lax.broadcasted_iota(jnp.int32, (block, block), 0)
+    c = lax.broadcasted_iota(jnp.int32, (block, block), 1)
+    cov_ref[...] = jnp.zeros_like(cov_ref)
+    for row, col, at in lower_blocks(size, block):
+        value = total_ref[at : at + block, :] * (1.0 / total_gates)
+        if row == col:
+            value = value + jnp.where(r == c, LOADING, 0.0)
+        cov_ref[row : row + block, col : col + block] = value
     transposed = (((1,), (1,)), ((), ()))
 
-    def step(index, carry):
-        start = pl.multiple_of(index * block, block)
-        here = pl.ds(start, block)
-        r = lax.broadcasted_iota(jnp.int32, (block, block), 0)
-        c = lax.broadcasted_iota(jnp.int32, (block, block), 1)
-        work_ref[:, :block] = cov_ref[here, here]
+    def dot(x, y):
+        return lax.dot_general(
+            x, y, transposed, precision=HIGHEST, preferred_element_type=jnp.float32
+        )
+
+    for start in range(0, size, block):
+        end = start + block
+        work_ref[:, :block] = cov_ref[start:end, start:end]
         work_ref[:, block:] = jnp.where(r == c, 1.0, 0.0)
         for first in range(0, block, PANEL):
             eliminate_panel(work_ref, first, block)
         inverse = work_ref[:, block:]
-        panel = lax.dot_general(
-            cov_ref[:, here], inverse, transposed, precision=HIGHEST,
-            preferred_element_type=jnp.float32,
-        )
-        below = lax.broadcasted_iota(jnp.int32, (size, block), 0) >= start + block
-        panel = jnp.where(below, panel, 0.0)
-        cov_ref[...] = cov_ref[...] - lax.dot_general(
-            panel, panel, transposed, precision=HIGHEST, preferred_element_type=jnp.float32
-        )
-        solved = lax.dot_general(
-            out_ref[:, here], inverse, transposed, precision=HIGHEST,
-            preferred_element_type=jnp.float32,
-        )
-        out_ref[...] = out_ref[...] - lax.dot_general(
-            solved, panel, transposed, precision=HIGHEST, preferred_element_type=jnp.float32
-        )
-        out_ref[:, here] = solved
-        return carry
-
-    lax.fori_loop(0, size // block, step, 0)
-
-
-def whiten(gram, snapshot, total_gates):
-    size = gram.shape[0]
+        solved = dot(out_ref[:, start:end], inverse)
+        out_ref[:, start:end] = solved
+        if end < size:
+            panel = dot(cov_ref[end:, start:end], inverse)
+            cov_ref[end:, end:] = cov_ref[end:, end:] - dot(panel, panel)
+            out_ref[:, end:] = out_ref[:, end:] - dot(solved, panel)
+
+
+def whiten_kernel(
+    total_gates, snapshot_ref, out_ref, part_ref, pair_ref, half_ref, inbox_ref, total_ref,
+    cov_ref, work_ref, *sems
+):
+    size = snapshot_ref.shape[1]
+    block = work_ref.shape[0]
+    for row in range(0, size, block):
+        gram = lax.dot_general(
+            snapshot_ref[:, row : row + block], snapshot_ref[:, : row + block],
+            (((0,), (0,)), ((), ())), precision=HIGHEST, preferred_element_type=jnp.float32,
+        )
+        for b_row, b_col, at in lower_blocks(size, block):
+            if b_row == row:
+                part_ref[at : at + block, :] = gram[:, b_col : b_col + block]
+    greet(range_partners())
+    sum_over_range(part_ref, pair_ref, half_ref, inbox_ref, total_ref, sems)
+    out_ref[...] = snapshot_ref[...]
+    factor_and_solve(total_gates, total_ref, out_ref, cov_ref, work_ref)
+
+
+def whiten_scratch(size, block, groups):
+    packed = len(lower_blocks(size, block)) * block
+    half = packed // 2
+    assert half % (8 * groups) == 0
+    dma = pltpu.SemaphoreType.DMA
+    others = max(groups - 1, 1)
+    return [
+        pltpu.VMEM((packed, block), jnp.float32),
+        pltpu.VMEM((half, block), jnp.float32),
+        pltpu.VMEM((half, block), jnp.float32),
+        pltpu.VMEM((others, half // groups, block), jnp.float32),
+        pltpu.VMEM((packed, block), jnp.float32),
+        pltpu.VMEM((size, size), jnp.float32),
+        pltpu.VMEM((block, 2 * block), jnp.float32),
+        dma, dma, dma((others,)), dma((others,)), dma((others,)), dma((others,)),
+        dma((groups,)), dma((groups,)),
+    ]
+
+
+def whiten(snapshot, total_gates):
+    size = snapshot.shape[1]
     block = min(BLOCK, size)
     return pl.pallas_call(
         functools.partial(whiten_kernel, total_gates),
         out_shape=jax.ShapeDtypeStruct(snapshot.shape, jnp.float32),
-        in_specs=[pl.BlockSpec(memory_space=pltpu.VMEM)] * 2,
+        in_specs=[pl.BlockSpec(memory_space=pltpu.VMEM)],
         out_specs=pl.BlockSpec(memory_space=pltpu.VMEM),
-        scratch_shapes=[
-            pltpu.VMEM((size, size), jnp.float32),
-            pltpu.VMEM((block, 2 * block), jnp.float32),
-        ],
-        compiler_params=pltpu.CompilerParams(vmem_limit_bytes=32 << 20),
+        scratch_shapes=whiten_scratch(size, block, lax.axis_size("range") // 2),
+        compiler_params=pltpu.CompilerParams(
+            vmem_limit_bytes=32 << 20, collective_id=1, has_side_effects=True
+        ),
         name="whiten",
-    )(gram, snapshot)
+    )(snapshot)
 
 
 def local(samples, taps, taper):
@@ -186,11 +296,7 @@
     )
     doppler = lax.all_to_all(spectrum, "pulse", split_axis=1, concat_axis=0, tiled=True)
     total_gates = gate_rows * range_devices
-    local_gram = lax.dot_general(
-        doppler, doppler, (((0,), (0,)), ((), ())), precision=lax.Precision.HIGHEST
-    )
-    summed = lax.psum(local_gram, "range")
-    return whiten(summed, doppler, total_gates)
+    return whiten(doppler, total_gates)
 
 
 def solution(mesh):

time: 249 us -> 182 us (0.73)
  waiting for transfers between devices: 108 us -> 50.4 us
  between operations: 13.5 us -> 0.1 us
  Pallas kernels: 31.4 us -> 39.3 us
  matrix products: 13.4 us -> 8.91 us
    psum x1 -> x0, waiting for transfers between devices: 57.3 us -> none  [local(): summed = lax.psum(local_gram, 'range')]
    pallas_call x1, Pallas kernels: 31.4 us -> 39.3 us  [whiten(): pl.pallas_call(functools.partial(whiten_kernel, total_gates), out_shape=j...]
    dot_general x1 -> x0, matrix products: 4.49 us -> none  [local(): lax.dot_general(doppler, doppler, (((0,), (0,)), ((), ())), precision=lax...]
  transfers between devices with their start and end apart: 4 -> 3, of which waited for: 3 -> 2; matrix products, arithmetic and copies ran while one was open for 1% -> 1% of each run, Pallas kernels for 0% -> 0%
where the time goes in v2:
time: 182 us
  blocking collectives  53.9 us (30%)
  waiting for transfers between devices  50.4 us (28%)
  Pallas kernels  39.3 us (22%)
  local copies, waits for them, and re-layouts  14.4 us (8%)
  matrix products  8.91 us (5%)
  starting transfers between devices  8.58 us (5%)
  other arithmetic  6.05 us (3%)
    all_to_all x1, blocking collectives, local(): lax.all_to_all(spectrum, 'pulse', split_axis=1, concat_axis=0, tiled=True)  53.9 us
    all_to_all x1, waiting for transfers between devices, local(): lax.all_to_all(tapered, 'pulse', split_axis=0, concat_axis=1, tiled=True)  48.3 us
    pallas_call x1, Pallas kernels, whiten(): pl.pallas_call(functools.partial(whiten_kernel, total_gates), out_shape=j...  39.3 us
    all_to_all x1, starting transfers between devices, local(): lax.all_to_all(tapered, 'pulse', split_axis=0, concat_axis=1, tiled=True)  4.88 us
    all_to_all x2, local copies, waits for them, and re-layouts, local(): lax.all_to_all(spectrum, 'pulse', split_axis=1, concat_axis=0, tiled=True)  4.58 us
    dot_general x1, matrix products, transform(): jnp.einsum('rpca,pabk->rkcb', arranged, doppler_table, precision=lax.Prec...  4.54 us
    dot_general x2, matrix products, local(): jnp.einsum('ab,ibj->iaj', band[:, part * tile_rows:(part + 1) * tile_rows...  4.37 us
  transfers between devices with their start and end apart: 3, of which 2 were waited for; matrix products, arithmetic and copies ran while one was open for 1% of the time, Pallas kernels for 0%

profile of v2, /device:TPU:0, one launch (start us, length us, event | category | flops | bytes accessed | tf_op | source)
XLA Modules:
  0.0 181.7 jit_solution(6781821911883086893)
XLA Ops:
  0.0 1.0 fusion.20
  1.0 2.4 %collective-permute-start = (f32[64,512]{1,0:T(8,128)S(1)}, f32[64,512]{1,0:T(8,128)S(1)}, u32[]{:S(2)}, u32[]{:S(2)}) collective-permute-start(f32[64,512]{1,0:T(8,128)S(1)} %get-tuple-element.7), channel_id=1, source_target_pairs={{0,4},{4,8},{8,12},{12,16},{16,20},{20,24},{24,28},{1,5},{5,9},{9,... | collective-permute-start | bytes 393224 | tf_op jit(solution)/shard_map/ppermute | solution.py:19
  3.4 1.3 collective-permute-start.1
  4.7 0.7 concatenate.14
  5.4 0.1 copy.12
  5.5 0.3 reshape.109
  5.8 0.7 broadcast_in_dim.2
  6.5 0.1 mul.119
  6.6 0.0 collective-permute-done
  6.6 2.1 %collective-permute-done.1 = f32[64,512]{1,0:T(8,128)S(1)} collective-permute-done((f32[64,512]{1,0:T(8,128)S(1)}, f32[64,512]{1,0:T(8,128)S(1)}, u32[]{:S(2)}, u32[]{:S(2)}) %collective-permute-start.1) | collective-permute-done | bytes 131104 | tf_op jit(solution)/shard_map/ppermute | solution.py:22
  8.7 2.6 %pad_maximum_fusion.1 = (f32[1024,512]{1,0:T(8,128)S(1)}, f32[1024,512]{1,0:T(8,128)S(1)}) fusion(f32[1024,512]{1,0:T(8,128)} %param.3, f32[64,512]{1,0:T(8,128)S(1)} %collective-permute-done, f32[64,512]{1,0:T(8,128)S(1)} %collective-permute-done.1), kind=kLoop, calls=%fused_computation.1 | loop fusion | flops 1048576 | bytes 6553600 | tf_op jit(solution)/shard_map/concatenate | solution.py:23
  11.4 2.1 %fusion.9 = f32[8,512,128]{1,2,0:T(8,128)S(1)} fusion(f32[8,128,512]{2,1,0:T(8,128)S(1)} %bitcast.47, f32[128,255]{1,0:T(8,128)S(1)} %reshape.109), kind=kOutput, calls=%fused_computation.13 | convolution fusion | flops 805306368 | bytes 4324864 | tf_op jit(solution)/shard_map/ab,ibj->iaj/dot_general | solution.py:284
  13.5 2.3 %convolution_add_fusion = f32[8,512,128]{1,2,0:T(8,128)S(1)} fusion(f32[8,512,128]{1,2,0:T(8,128)S(1)} %fusion.9, f32[8,128,512]{2,1,0:T(8,128)S(1)} %bitcast.46, f32[128,255]{1,0:T(8,128)S(1)} %reshape.109), kind=kOutput, calls=%fused_computation.6 | convolution fusion | flops 805830656 | bytes 6356992 | tf_op jit(solution)/shard_map/ab,ibj->iaj/dot_general | solution.py:284
  15.7 1.8 copy.6
  17.6 3.1 %broadcast_multiply_fusion = f32[4,256,512]{1,2,0:T(8,128)} fusion(f32[4,256,512]{1,2,0:T(8,128)} %copy.6, f32[512]{0:T(512)S(1)} %mul.119), kind=kLoop, calls=%fused_computation.7 | loop fusion | flops 524288 | bytes 4196352 | tf_op jit(solution)/shard_map/mul | solution.py:291
  20.7 4.9 %all-to-all-start = ((f32[4,256,512]{1,2,0:T(8,128)}), f32[4,256,512]{1,2,0:T(8,128)S(1)}, u32[]{:S(2)}, u32[]{:S(2)}) async-start(f32[4,256,512]{1,2,0:T(8,128)} %broadcast_multiply_fusion), calls=%async_computation | async-start | bytes 4194304 | tf_op jit(solution)/shard_map/all_to_all | solution.py:293
  25.6 0.1 fusion.17
  25.7 0.2 sine_multiply_fusion
  25.9 48.3 %all-to-all-done = f32[4,256,512]{1,2,0:T(8,128)S(1)} async-done(((f32[4,256,512]{1,2,0:T(8,128)}), f32[4,256,512]{1,2,0:T(8,128)S(1)}, u32[]{:S(2)}, u32[]{:S(2)}) %all-to-all-start) | async-done | bytes 2097184 | tf_op jit(solution)/shard_map/all_to_all | solution.py:293
  74.2 2.2 %reshape.111 = f32[256,64,16,2]{0,3,2,1:T(2,128)} reshape(f32[256,4,512]{0,2,1:T(8,128)S(1)} %bitcast.49) | data formatting | bytes 4194304 | tf_op jit(solution)/shard_map/reshape | solution.py:48
  76.4 4.5 %fusion.3 = f32[256,64,16,2]{0,1,2,3:T(8,128)S(1)} fusion(f32[256,64,16,2]{0,3,2,1:T(2,128)} %reshape.111, f32[64,1,2,64]{0,3,1,2:T(8,128)S(1)} %get-tuple-element.10, f32[64,1,2,64]{0,3,1,2:T(8,128)S(1)} %get-tuple-element.9), kind=kOutput, calls=%fused_computation.5 | convolution fusion | flops 805322752 | bytes 4259840 | tf_op jit(solution)/shard_map/rpca,pabk->rkcb/dot_general | solution.py:49
  80.9 1.6 copy.8
  82.6 2.4 %all_to_all.26 = f32[256,4,512]{0,2,1:T(8,128)} reshape(f32[256,64,16,2]{0,3,2,1:T(2,128)S(1)} %copy.8) | data formatting | bytes 4194304 | tf_op jit(solution)/shard_map/all_to_all | solution.py:297
  85.0 53.9 %all_to_all.32 = f32[256,4,512]{0,2,1:T(8,128)} all-to-all(f32[256,4,512]{0,2,1:T(8,128)} %all_to_all.26), channel_id=1, replica_groups=mesh['range'=8,'pulse'=4] {'pulse'}, dimensions={1} | all-to-all | bytes 4194304 | tf_op jit(solution)/shard_map/all_to_all | solution.py:297
  139.0 2.1 %copy.9 = f32[4,256,512]{2,1,0:T(8,128)S(1)} copy(f32[4,256,512]{1,2,0:T(8,128)} %bitcast.50) | data formatting | bytes 4194304 | tf_op jit(solution)/shard_map/all_to_all | solution.py:297
  141.1 39.3 %whiten.1 = f32[1024,512]{1,0:T(8,128)S(1)} custom-call(f32[1024,512]{1,0:T(8,128)S(1)} %bitcast.45), custom_call_target="tpu_custom_call" | custom-call | tf_op jit(solution)/shard_map/whiten/pallas_call | solution.py:253
  180.4 1.3 copy.20
  (2 shorter events, 0.0 us)
Async XLA Ops:
  1.0 5.6 %collective-permute-start = (f32[64,512]{1,0:T(8,128)S(1)}, f32[64,512]{1,0:T(8,128)S(1)}, u32[]{:S(2)}, u32[]{:S(2)}) collective-permute-start(f32[64,512]{1,0:T(8,128)S(1)} %get-tuple-element.7), channel_id=1, source_target_pairs={{0,4},{4,8},{8,12},{12,16},{16,20},{20,24},{24,28},{1,5},{5,9},{9,... | collective-permute-start | bytes 393224 | tf_op jit(solution)/shard_map/ppermute | solution.py:19
  3.4 5.3 %collective-permute-start.1 = (f32[64,512]{1,0:T(8,128)S(1)}, f32[64,512]{1,0:T(8,128)S(1)}, u32[]{:S(2)}, u32[]{:S(2)}) collective-permute-start(f32[64,512]{1,0:T(8,128)S(1)} %get-tuple-element.8), channel_id=1, source_target_pairs={{4,0},{8,4},{12,8},{16,12},{20,16},{24,20},{28,24},{5,1},{9,5},{13... | collective-permute-start | bytes 393224 | tf_op jit(solution)/shard_map/ppermute | solution.py:22
  20.7 53.5 %all-to-all-start = ((f32[4,256,512]{1,2,0:T(8,128)}), f32[4,256,512]{1,2,0:T(8,128)S(1)}, u32[]{:S(2)}, u32[]{:S(2)}) async-start(f32[4,256,512]{1,2,0:T(8,128)} %broadcast_multiply_fusion), calls=%async_computation | async-start | bytes 4194304 | tf_op jit(solution)/shard_map/all_to_all | solution.py:293

commit v3 on v2

--- a/solution.py
+++ b/solution.py
@@ -3,6 +3,7 @@
 
 import jax
 import jax.numpy as jnp
+import numpy as np
 from jax import lax
 from jax.experimental import pallas as pl
 from jax.experimental.pallas import tpu as pltpu
@@ -11,49 +12,10 @@
 LOADING = 0.05
 
 
-def padded_2(block, sides, width):
-    for axis, dim in sides:
-        count = lax.axis_size(axis)
-        forward = [(i, i + 1) for i in range(count - 1)]
-        backward = [(target, source) for source, target in forward]
-        low = lax.ppermute(
-            lax.slice_in_dim(block, block.shape[dim] - width, None, axis=dim), axis, forward
-        )
-        high = lax.ppermute(lax.slice_in_dim(block, 0, width, axis=dim), axis, backward)
-        block = jnp.concatenate([low, block, high], axis=dim)
-    return block
-
-
-def toeplitz(taps, tile_rows):
-    tap_count = taps.shape[0]
-    padded_taps = jnp.concatenate([taps, jnp.zeros((tile_rows,), taps.dtype)])
-    repeated = jnp.tile(padded_taps, tile_rows)[: tile_rows * (tap_count + tile_rows - 1)]
-    return repeated.reshape(tile_rows, tap_count + tile_rows - 1)
-
-
-def doppler_matrix(pulses):
-    position = jnp.arange(pulses, dtype=jnp.int32)
-    phase_index = position[:, None] * position[None, :] % pulses
-    angles = phase_index.astype(jnp.float32) * (2.0 * math.pi / pulses)
-    amplitude = 1.0 / math.sqrt(pulses)
-    cosine = jnp.cos(angles) * amplitude
-    sine_part = jnp.sin(angles) * amplitude
-    real_in = jnp.stack([cosine, -sine_part], axis=1)
-    imag_in = jnp.stack([sine_part, cosine], axis=1)
-    return jnp.stack([real_in, imag_in], axis=1)
-
-
-def transform(received, doppler_table, pulses, group_width):
-    part_rows = received.shape[0]
-    arranged = received.reshape(part_rows, pulses, group_width // 2, 2)
-    spectrum = jnp.einsum(
-        "rpca,pabk->rkcb", arranged, doppler_table, precision=lax.Precision.HIGHEST
-    )
-    return spectrum.reshape(part_rows, pulses, group_width)
-
-
 BLOCK = 128
 PANEL = 16
+LANES = 128
+CHUNKS = 4
 HIGHEST = lax.Precision.HIGHEST
 
 
@@ -208,10 +170,179 @@
             out_ref[:, end:] = out_ref[:, end:] - dot(solved, panel)
 
 
-def whiten_kernel(
-    total_gates, snapshot_ref, out_ref, part_ref, pair_ref, half_ref, inbox_ref, total_ref,
-    cov_ref, work_ref, *sems
+def quarter_turn(x):
+    lane = lax.broadcasted_iota(jnp.int32, x.shape, 1)
+    width = x.shape[1]
+    return jnp.where(
+        lane % 2 == 0, pltpu.roll(x, width - 1, axis=1), -pltpu.roll(x, 1, axis=1)
+    )
+
+
+def doppler_constants(pulses, devices, group):
+    bins = pulses // devices
+    lane = np.arange(bins * group)
+    turn = (lane // group)[None, :] * np.arange(devices)[:, None] % pulses
+    angle = turn * (2.0 * math.pi / pulses)
+    first = np.arange(bins)
+    phase = (first[:, None] * first[None, :] % bins) * (2.0 * math.pi / bins)
+    cosine, sine = np.cos(phase), np.sin(phase)
+    pair = np.stack(
+        [np.stack([cosine, -sine], axis=-1), np.stack([sine, cosine], axis=-1)], axis=1
+    ) / math.sqrt(pulses)
+    table = np.einsum("paqb,cd->pcaqdb", pair, np.eye(group // 2))
+    table = table.reshape(bins * group, bins * group)
+    return tuple(np.asarray(v, np.float32) for v in (np.cos(angle), np.sin(angle), table))
+
+
+def transform_chunk(rows, group, gathered_ref, cos_ref, sin_ref, table_ref, stage_ref, spread_ref):
+    devices, _, width = gathered_ref.shape
+    count = rows.size
+    bins = width // group
+    for at in range(0, width, LANES):
+        lanes = slice(at, at + LANES)
+        parts = [gathered_ref[z, rows, lanes] for z in range(devices)]
+        turned = [quarter_turn(x) for x in parts]
+        for k in range(devices):
+            total = None
+            for z in range(devices):
+                step = z * k % devices
+                for weight, term in (
+                    (math.cos(2.0 * math.pi * step / devices), parts[z]),
+                    (math.sin(2.0 * math.pi * step / devices), turned[z]),
+                ):
+                    if abs(weight) < 1e-9:
+                        continue
+                    sign = 1.0 if weight > 0 else -1.0
+                    if abs(abs(weight) - 1.0) > 1e-9:
+                        term, sign = term * weight, 1.0
+                    if total is None:
+                        total = term if sign > 0 else -term
+                    else:
+                        total = total + term if sign > 0 else total - term
+            total = total * cos_ref[k : k + 1, lanes] + quarter_turn(total) * sin_ref[
+                k : k + 1, lanes
+            ]
+            stage_ref[k * count : (k + 1) * count, lanes] = total
+    mixed = jnp.dot(
+        stage_ref[...], table_ref[...], precision=HIGHEST, preferred_element_type=jnp.float32
+    )
+    place = lax.broadcasted_iota(jnp.int32, (count, LANES), 1) // group
+    for target in range(devices):
+        for at in range(0, width, LANES):
+            out = None
+            for n in range(LANES // group):
+                k = target * bins + at // group + n
+                low, high = k % devices, k // devices
+                source = high * group
+                block = source // LANES * LANES
+                piece = mixed[low * count : (low + 1) * count, block : block + LANES]
+                shift = (n * group - source) % LANES
+                if shift:
+                    piece = pltpu.roll(piece, shift, axis=1)
+                out = piece if out is None else jnp.where(place == n, piece, out)
+            spread_ref[target, rows, at : at + LANES] = out
+
+
+def exchange(
+    samples_ref, taps_ref, taper_ref, cos_ref, sin_ref, table_ref, snapshot_ref,
+    low_ref, high_ref, padded_ref, outgoing_ref, gathered_ref, stage_ref, spread_ref, group, sems
 ):
+    halo_send, halo_recv, in_send, in_recv, back_send, back_recv = sems
+    gates, width = samples_ref.shape
+    devices, share, _ = gathered_ref.shape
+    half = low_ref.shape[0]
+    count = share // CHUNKS
+    z = lax.axis_index("pulse")
+    me, ranges = lax.axis_index("range"), lax.axis_size("range")
+
+    def send(src, dst, send_sem, recv_sem, axis, target):
+        copy = pltpu.make_async_remote_copy(
+            src_ref=src, dst_ref=dst, send_sem=send_sem, recv_sem=recv_sem,
+            device_id={axis: target}, device_id_type=pl.DeviceIdType.MESH,
+        )
+        copy.start()
+        return copy
+
+    halos = [
+        send(
+            samples_ref.at[gates - half :], low_ref, halo_send.at[0], halo_recv.at[0],
+            "range", lax.rem(me + 1, ranges),
+        ),
+        send(
+            samples_ref.at[:half], high_ref, halo_send.at[1], halo_recv.at[1],
+            "range", lax.rem(me + ranges - 1, ranges),
+        ),
+    ]
+    padded_ref[half : half + gates, :] = samples_ref[...]
+    taps = jnp.broadcast_to(taps_ref[...], (count, taps_ref.shape[1]))
+    span = count + 2 * half
+    band = pltpu.roll(taps, 0, axis=1, stride=1, stride_axis=0)[:, :span]
+    for copy in halos:
+        copy.wait_recv()
+    padded_ref[:half, :] = jnp.where(me > 0, low_ref[...], 0.0)
+    padded_ref[half + gates :, :] = jnp.where(me < ranges - 1, high_ref[...], 0.0)
+    shifts = sorted(range(1, devices), key=lambda s: abs(2 * s - devices))
+    ins = {}
+    for part in range(CHUNKS):
+        for shift in shifts + [0]:
+            target = lax.rem(z + shift, devices)
+            start = pl.multiple_of(target * share + part * count, 8)
+            value = taper_ref[...] * jnp.dot(
+                band, padded_ref[pl.ds(start, span), :], precision=HIGHEST,
+                preferred_element_type=jnp.float32,
+            )
+            rows = pl.ds(part * count, count)
+            if shift == 0:
+                gathered_ref[z, rows, :] = value
+                continue
+            here = outgoing_ref.at[pl.ds(start, count)]
+            here[...] = value
+            ins[part, shift] = send(
+                here, gathered_ref.at[z, rows], in_send.at[shift - 1, part],
+                in_recv.at[shift - 1, part], "pulse", target,
+            )
+    backs = []
+    for part in range(CHUNKS):
+        rows = pl.ds(part * count, count)
+        for shift in shifts:
+            ins[part, shift].wait_recv()
+        transform_chunk(
+            rows, group, gathered_ref, cos_ref, sin_ref, table_ref, stage_ref, spread_ref
+        )
+        home = pl.ds(pl.multiple_of(z * share + part * count, 8), count)
+        for shift in shifts:
+            target = lax.rem(z + shift, devices)
+            backs.append(
+                send(
+                    spread_ref.at[target, rows], snapshot_ref.at[home],
+                    back_send.at[shift - 1, part], back_recv.at[shift - 1, part],
+                    "pulse", target,
+                )
+            )
+        snapshot_ref[home, :] = spread_ref[z, rows, :]
+    for copy in backs:
+        copy.wait_recv()
+    for copy in halos + list(ins.values()) + backs:
+        copy.wait_send()
+
+
+def whole_kernel(
+    total_gates, group, samples_ref, taps_ref, taper_ref, cos_ref, sin_ref, table_ref, out_ref,
+    snapshot_ref, low_ref, high_ref, padded_ref, outgoing_ref, gathered_ref, stage_ref,
+    spread_ref, part_ref, pair_ref, half_ref, inbox_ref, total_ref, cov_ref, work_ref, *sems
+):
+    z, devices = lax.axis_index("pulse"), lax.axis_size("pulse")
+    me, ranges = lax.axis_index("range"), lax.axis_size("range")
+    greet(
+        range_partners()
+        + [("range", lax.rem(me + 1, ranges)), ("range", lax.rem(me + ranges - 1, ranges))]
+        + [("pulse", lax.rem(z + shift, devices)) for shift in range(1, devices)]
+    )
+    exchange(
+        samples_ref, taps_ref, taper_ref, cos_ref, sin_ref, table_ref, snapshot_ref,
+        low_ref, high_ref, padded_ref, outgoing_ref, gathered_ref, stage_ref, spread_ref, group,
+        sems[:6],
+    )
     size = snapshot_ref.shape[1]
     block = work_ref.shape[0]
     for row in range(0, size, block):
@@ -222,8 +353,7 @@
         for b_row, b_col, at in lower_blocks(size, block):
             if b_row == row:
                 part_ref[at : at + block, :] = gram[:, b_col : b_col + block]
-    greet(range_partners())
-    sum_over_range(part_ref, pair_ref, half_ref, inbox_ref, total_ref, sems)
+    sum_over_range(part_ref, pair_ref, half_ref, inbox_ref, total_ref, sems[6:])
     out_ref[...] = snapshot_ref[...]
     factor_and_solve(total_gates, total_ref, out_ref, cov_ref, work_ref)
 
@@ -242,61 +372,50 @@
         pltpu.VMEM((packed, block), jnp.float32),
         pltpu.VMEM((size, size), jnp.float32),
         pltpu.VMEM((block, 2 * block), jnp.float32),
+    ], [
         dma, dma, dma((others,)), dma((others,)), dma((others,)), dma((others,)),
         dma((groups,)), dma((groups,)),
     ]
 
 
-def whiten(snapshot, total_gates):
-    size = snapshot.shape[1]
-    block = min(BLOCK, size)
+def local(samples, taps, taper):
+    gates, width = samples.shape
+    tap_count = taps.shape[0]
+    half = tap_count // 2
+    bins = taper.shape[0]
+    devices, ranges = lax.axis_size("pulse"), lax.axis_size("range")
+    group = width // bins
+    share = gates // devices
+    count = share // CHUNKS
+    block = min(BLOCK, width)
+    cosine, sine, table = doppler_constants(bins * devices, devices, group)
+    room = -(-(tap_count + count) // LANES) * LANES
+    padded_taps = jnp.pad(taps, (0, room - tap_count))[None, :]
+    taper_row = jnp.repeat(taper, group)[None, :]
+    buffers, sems = whiten_scratch(width, block, ranges // 2)
+    dma = pltpu.SemaphoreType.DMA
+    own = [
+        pltpu.VMEM((gates, width), jnp.float32),
+        pltpu.VMEM((half, width), jnp.float32),
+        pltpu.VMEM((half, width), jnp.float32),
+        pltpu.VMEM((gates + 2 * half, width), jnp.float32),
+        pltpu.VMEM((gates, width), jnp.float32),
+        pltpu.VMEM((devices, share, width), jnp.float32),
+        pltpu.VMEM((devices * count, width), jnp.float32),
+        pltpu.VMEM((devices, share, width), jnp.float32),
+    ]
+    pulse_sems = [dma((2,)), dma((2,))] + [dma((devices - 1, CHUNKS))] * 4
     return pl.pallas_call(
-        functools.partial(whiten_kernel, total_gates),
-        out_shape=jax.ShapeDtypeStruct(snapshot.shape, jnp.float32),
-        in_specs=[pl.BlockSpec(memory_space=pltpu.VMEM)],
+        functools.partial(whole_kernel, gates * ranges, group),
+        out_shape=jax.ShapeDtypeStruct(samples.shape, jnp.float32),
+        in_specs=[pl.BlockSpec(memory_space=pltpu.VMEM)] * 6,
         out_specs=pl.BlockSpec(memory_space=pltpu.VMEM),
-        scratch_shapes=whiten_scratch(size, block, lax.axis_size("range") // 2),
+        scratch_shapes=own + buffers + pulse_sems + sems,
         compiler_params=pltpu.CompilerParams(
-            vmem_limit_bytes=32 << 20, collective_id=1, has_side_effects=True
+            vmem_limit_bytes=48 << 20, collective_id=1, has_side_effects=True
         ),
         name="whiten",
-    )(snapshot)
-
-
-def local(samples, taps, taper):
-    gate_rows, columns = samples.shape
-    tap_count = taps.shape[0]
-    half_taps = tap_count // 2
-    bin_count = taper.shape[0]
-    pulse_devices = lax.axis_size("pulse")
-    range_devices = lax.axis_size("range")
-    pulses = bin_count * pulse_devices
-    channels = columns // (2 * bin_count)
-    padded = padded_2(samples, (("range", 0),), half_taps)
-    tile_rows = min(128, gate_rows)
-    matrix = toeplitz(taps, tile_rows)
-
-    band = jnp.concatenate([matrix, jnp.zeros((tile_rows, 1), matrix.dtype)], axis=1)
-    tiles = padded.reshape(-1, tile_rows, columns)
-    span = gate_rows // tile_rows
-    compressed = 0.0
-    for part in range(band.shape[1] // tile_rows):
-        compressed = compressed + jnp.einsum(
-            "ab,ibj->iaj",
-            band[:, part * tile_rows : (part + 1) * tile_rows],
-            tiles[part : part + span],
-            precision=HIGHEST,
-        )
-    compressed = compressed.reshape(gate_rows, columns)
-    tapered = compressed * jnp.repeat(taper, 2 * channels)[None, :]
-    doppler_table = doppler_matrix(pulses)
-    gathered = lax.all_to_all(tapered, "pulse", split_axis=0, concat_axis=1, tiled=True)
-    spectrum = transform(gathered, doppler_table, pulses, 2 * channels).reshape(
-        gathered.shape[0], pulses * 2 * channels
-    )
-    doppler = lax.all_to_all(spectrum, "pulse", split_axis=1, concat_axis=0, tiled=True)
-    total_gates = gate_rows * range_devices
-    return whiten(doppler, total_gates)
+    )(samples, padded_taps, taper_row, cosine, sine, table)
 
 
 def solution(mesh):

time: 182 us -> 143 us (0.79)
  Pallas kernels: 39.3 us -> 135 us
  blocking collectives: 53.9 us -> 0 us
  waiting for transfers between devices: 50.4 us -> 0 us
  matrix products: 8.91 us -> 0 us
  starting transfers between devices: 8.58 us -> 0 us
  local copies, waits for them, and re-layouts: 14.4 us -> 6.99 us
  other arithmetic: 6.05 us -> 0 us
    pallas_call x1, Pallas kernels: 39.3 us -> 135 us  [local(): pl.pallas_call(functools.partial(whole_kernel, gates * ranges, group), ou...]
    all_to_all x1 -> x0, blocking collectives: 53.9 us -> none  [local(): lax.all_to_all(spectrum, 'pulse', split_axis=1, concat_axis=0, tiled=True)]
    all_to_all x1 -> x0, waiting for transfers between devices: 48.3 us -> none  [local(): lax.all_to_all(tapered, 'pulse', split_axis=0, concat_axis=1, tiled=True)]
    dot_general x3 -> x0, matrix products: 8.91 us -> none  [the longest x1 4.54 us: transform(): jnp.einsum('rpca,pabk->rkcb', arranged, doppler_table, precision=lax.Prec...]
    all_to_all x1 -> x0, starting transfers between devices: 4.88 us -> none  [local(): lax.all_to_all(tapered, 'pulse', split_axis=0, concat_axis=1, tiled=True)]
    all_to_all x2 -> x0, local copies, waits for them, and re-layouts: 4.58 us -> none  [local(): lax.all_to_all(spectrum, 'pulse', split_axis=1, concat_axis=0, tiled=True)]
    reshape x3 -> x0, local copies, waits for them, and re-layouts: 4.36 us -> none  [the longest x1 2.22 us: transform(): arranged = received.reshape(part_rows, pulses, group_width // 2, 2)]
    unnamed x3 -> x9, local copies, waits for them, and re-layouts: 1.4 us -> 5.53 us
  transfers between devices with their start and end apart: 3 -> 0, of which waited for: 2 -> 0; matrix products, arithmetic and copies ran while one was open for 1% -> 0% of each run, Pallas kernels for 0% -> 0%
where the time goes in v3:
time: 143 us; the launch traced here: 142 us
  Pallas kernels  135 us (94%)
  local copies, waits for them, and re-layouts  6.99 us (5%)
    pallas_call x1, Pallas kernels, local(): pl.pallas_call(functools.partial(whole_kernel, gates * ranges, group), ou...  135 us
    unnamed x9, local copies, waits for them, and re-layouts  5.53 us

profile of v3, /device:TPU:0, one launch (start us, length us, event | category | flops | bytes accessed | tf_op | source)
XLA Modules:
  0.0 142.1 jit_solution(10245575601899038158)
XLA Ops:
  0.0 0.7 pad.4
  0.7 0.7 broadcast_in_dim.7
  1.4 0.1 broadcast_in_dim_reshape.3.taper_ref
  1.5 0.0 copy-start
  1.5 1.6 %copy-done = f32[1024,512]{1,0:T(8,128)S(1)} copy-done((f32[1024,512]{1,0:T(8,128)S(1)}, f32[1024,512]{1,0:T(8,128)}, u32[]{:S(2)}) %copy-start) | copy-done | bytes 2097176
  3.1 0.0 copy-start.1
  3.1 1.2 copy-done.1
  4.3 0.0 copy-start.2
  4.3 0.7 copy-done.2
  5.0 0.0 copy-start.3
  5.0 0.7 copy-done.3
  5.7 135.1 %whiten.1 = f32[1024,512]{1,0:T(8,128)S(1)} custom-call(f32[1024,512]{1,0:T(8,128)S(1)} %copy-done, f32[1,256]{1,0:T(1,128)S(1)} %bitcast.1, f32[1,512]{1,0:T(1,128)S(1)} %broadcast_in_dim_reshape.3.taper_ref, f32[4,512]{1,0:T(4,128)S(1)} %copy-done.3, f32[4,512]{1,0:T(4,128)S(1)} %copy-done.2, f32[512,512]{1,0:T(8,128)S(1)} %copy-done.1), custom_call_target="tpu_custom_call" | custom-call | tf_op jit(solution)/shard_map/whiten/pallas_call | solution.py:408
  140.8 1.3 copy.8
Async XLA Ops:
  1.5 1.6 %copy-start = (f32[1024,512]{1,0:T(8,128)S(1)}, f32[1024,512]{1,0:T(8,128)}, u32[]{:S(2)}) copy-start(f32[1024,512]{1,0:T(8,128)} %samples_ref.1) | copy-start | bytes 6291460
  3.1 1.2 copy-start.1
  4.3 0.7 copy-start.2
  5.0 0.7 copy-start.3

commit v4 on v3

--- a/solution.py
+++ b/solution.py
@@ -137,37 +137,56 @@
     return found
 
 
-def factor_and_solve(total_gates, total_ref, out_ref, cov_ref, work_ref):
+def factor_and_solve(
+    total_gates, total_ref, data_ref, cov_ref, work_ref, inverse_ref, panel_ref, emit
+):
     size = cov_ref.shape[0]
     block = work_ref.shape[0]
     r = lax.broadcasted_iota(jnp.int32, (block, block), 0)
     c = lax.broadcasted_iota(jnp.int32, (block, block), 1)
-    cov_ref[...] = jnp.zeros_like(cov_ref)
     for row, col, at in lower_blocks(size, block):
         value = total_ref[at : at + block, :] * (1.0 / total_gates)
         if row == col:
             value = value + jnp.where(r == c, LOADING, 0.0)
+        else:
+            cov_ref[col : col + block, row : row + block] = jnp.zeros_like(value)
         cov_ref[row : row + block, col : col + block] = value
     transposed = (((1,), (1,)), ((), ()))
+    piece = data_ref.shape[0] // CHUNKS
 
     def dot(x, y):
         return lax.dot_general(
             x, y, transposed, precision=HIGHEST, preferred_element_type=jnp.float32
         )
 
+    def solve_piece(start, part):
+        end = start + block
+        rows = slice(part * piece, (part + 1) * piece)
+        solved = dot(data_ref[rows, start:end], inverse_ref[...])
+        data_ref[rows, start:end] = solved
+        if end < size:
+            data_ref[rows, end:] = data_ref[rows, end:] - dot(solved, panel_ref[: size - end, :])
+        emit(start // block, part)
+
+    waiting = []
     for start in range(0, size, block):
         end = start + block
         work_ref[:, :block] = cov_ref[start:end, start:end]
         work_ref[:, block:] = jnp.where(r == c, 1.0, 0.0)
-        for first in range(0, block, PANEL):
+        for number, first in enumerate(range(0, block, PANEL)):
             eliminate_panel(work_ref, first, block)
-        inverse = work_ref[:, block:]
-        solved = dot(out_ref[:, start:end], inverse)
-        out_ref[:, start:end] = solved
+            if waiting and number % 2 == 0:
+                solve_piece(*waiting.pop(0))
+        while waiting:
+            solve_piece(*waiting.pop(0))
+        inverse_ref[...] = work_ref[:, block:]
         if end < size:
-            panel = dot(cov_ref[end:, start:end], inverse)
+            panel = dot(cov_ref[end:, start:end], work_ref[:, block:])
+            panel_ref[: size - end, :] = panel
             cov_ref[end:, end:] = cov_ref[end:, end:] - dot(panel, panel)
-            out_ref[:, end:] = out_ref[:, end:] - dot(solved, panel)
+        waiting = [(start, part) for part in range(CHUNKS)]
+    for item in waiting:
+        solve_piece(*item)
 
 
 def quarter_turn(x):
@@ -194,7 +213,7 @@
     return tuple(np.asarray(v, np.float32) for v in (np.cos(angle), np.sin(angle), table))
 
 
-def transform_chunk(rows, group, gathered_ref, cos_ref, sin_ref, table_ref, stage_ref, spread_ref):
+def transform_chunk(rows, group, gathered_ref, const_ref, stage_ref, spread_ref):
     devices, _, width = gathered_ref.shape
     count = rows.size
     bins = width // group
@@ -219,12 +238,12 @@
                         total = term if sign > 0 else -term
                     else:
                         total = total + term if sign > 0 else total - term
-            total = total * cos_ref[k : k + 1, lanes] + quarter_turn(total) * sin_ref[
-                k : k + 1, lanes
-            ]
+            total = total * const_ref[width + k : width + k + 1, lanes] + quarter_turn(
+                total
+            ) * const_ref[width + devices + k : width + devices + k + 1, lanes]
             stage_ref[k * count : (k + 1) * count, lanes] = total
     mixed = jnp.dot(
-        stage_ref[...], table_ref[...], precision=HIGHEST, preferred_element_type=jnp.float32
+        stage_ref[...], const_ref[:width, :], precision=HIGHEST, preferred_element_type=jnp.float32
     )
     place = lax.broadcasted_iota(jnp.int32, (count, LANES), 1) // group
     for target in range(devices):
@@ -244,8 +263,8 @@
 
 
 def exchange(
-    samples_ref, taps_ref, taper_ref, cos_ref, sin_ref, table_ref, snapshot_ref,
-    low_ref, high_ref, padded_ref, outgoing_ref, gathered_ref, stage_ref, spread_ref, group, sems
+    samples_ref, taps_ref, taper_ref, load, load_const, const_ref, snapshot_ref, low_ref, high_ref,
+    padded_ref, outgoing_ref, gathered_ref, stage_ref, spread_ref, group, sems, use_part
 ):
     halo_send, halo_recv, in_send, in_recv, back_send, back_recv = sems
     gates, width = samples_ref.shape
@@ -273,21 +292,37 @@
             "range", lax.rem(me + ranges - 1, ranges),
         ),
     ]
-    padded_ref[half : half + gates, :] = samples_ref[...]
-    taps = jnp.broadcast_to(taps_ref[...], (count, taps_ref.shape[1]))
+    tap_count = taps_ref.shape[1]
+    room = -(-(tap_count + count) // LANES) * LANES
+    taps = jnp.concatenate(
+        [taps_ref[...], jnp.zeros((1, room - tap_count), jnp.float32)], axis=1
+    )
     span = count + 2 * half
-    band = pltpu.roll(taps, 0, axis=1, stride=1, stride_axis=0)[:, :span]
-    for copy in halos:
-        copy.wait_recv()
-    padded_ref[:half, :] = jnp.where(me > 0, low_ref[...], 0.0)
-    padded_ref[half + gates :, :] = jnp.where(me < ranges - 1, high_ref[...], 0.0)
+    band = pltpu.roll(
+        jnp.broadcast_to(taps, (count, room)), 0, axis=1, stride=1, stride_axis=0
+    )[:, :span]
+    pulse = lax.broadcasted_iota(jnp.int32, (1, width), 1) // group
+    taper = jnp.zeros((1, width), jnp.float32)
+    for p in range(width // group):
+        taper = jnp.where(pulse == p, taper_ref[p], taper)
+    inner = [
+        p for p in range(CHUNKS) if p * count >= half and share - (p + 1) * count >= half
+    ]
+    outer = [p for p in range(CHUNKS) if p not in inner]
+    order = inner + outer
     shifts = sorted(range(1, devices), key=lambda s: abs(2 * s - devices))
     ins = {}
-    for part in range(CHUNKS):
+    load.wait()
+    for part in order:
+        if part == outer[0]:
+            for copy in halos:
+                copy.wait_recv()
+            padded_ref[:half, :] = jnp.where(me > 0, low_ref[...], 0.0)
+            padded_ref[half + gates :, :] = jnp.where(me < ranges - 1, high_ref[...], 0.0)
         for shift in shifts + [0]:
             target = lax.rem(z + shift, devices)
             start = pl.multiple_of(target * share + part * count, 8)
-            value = taper_ref[...] * jnp.dot(
+            value = taper * jnp.dot(
                 band, padded_ref[pl.ds(start, span), :], precision=HIGHEST,
                 preferred_element_type=jnp.float32,
             )
@@ -301,61 +336,93 @@
                 here, gathered_ref.at[z, rows], in_send.at[shift - 1, part],
                 in_recv.at[shift - 1, part], "pulse", target,
             )
-    backs = []
-    for part in range(CHUNKS):
+    load_const.wait()
+    backs = {}
+    for part in order:
         rows = pl.ds(part * count, count)
         for shift in shifts:
             ins[part, shift].wait_recv()
-        transform_chunk(
-            rows, group, gathered_ref, cos_ref, sin_ref, table_ref, stage_ref, spread_ref
-        )
-        home = pl.ds(pl.multiple_of(z * share + part * count, 8), count)
+        transform_chunk(rows, group, gathered_ref, const_ref, stage_ref, spread_ref)
+        home = pl.ds(pl.multiple_of((part * devices + z) * count, 8), count)
         for shift in shifts:
             target = lax.rem(z + shift, devices)
-            backs.append(
-                send(
-                    spread_ref.at[target, rows], snapshot_ref.at[home],
-                    back_send.at[shift - 1, part], back_recv.at[shift - 1, part],
-                    "pulse", target,
-                )
+            backs[part, shift] = send(
+                spread_ref.at[target, rows], snapshot_ref.at[home],
+                back_send.at[shift - 1, part], back_recv.at[shift - 1, part],
+                "pulse", target,
             )
         snapshot_ref[home, :] = spread_ref[z, rows, :]
-    for copy in backs:
-        copy.wait_recv()
-    for copy in halos + list(ins.values()) + backs:
-        copy.wait_send()
+    for part in order:
+        for shift in shifts:
+            backs[part, shift].wait_recv()
+        use_part(part, part == order[0])
+    return halos + list(ins.values()) + list(backs.values())
 
 
 def whole_kernel(
-    total_gates, group, samples_ref, taps_ref, taper_ref, cos_ref, sin_ref, table_ref, out_ref,
+    total_gates, group, samples_ref, taps_ref, taper_ref, given_ref, out_ref,
     snapshot_ref, low_ref, high_ref, padded_ref, outgoing_ref, gathered_ref, stage_ref,
-    spread_ref, part_ref, pair_ref, half_ref, inbox_ref, total_ref, cov_ref, work_ref, *sems
+    spread_ref, const_ref, inverse_ref, panel_ref, part_ref, pair_ref, half_ref, inbox_ref,
+    total_ref, cov_ref, work_ref, load_sem, const_sem, out_sem, *sems
 ):
     z, devices = lax.axis_index("pulse"), lax.axis_size("pulse")
     me, ranges = lax.axis_index("range"), lax.axis_size("range")
+    gates, size = samples_ref.shape
+    block = work_ref.shape[0]
+    half = low_ref.shape[0]
+    load = pltpu.make_async_copy(samples_ref, padded_ref.at[half : half + gates], load_sem)
+    load.start()
+    load_const = pltpu.make_async_copy(given_ref, const_ref, const_sem)
+    load_const.start()
     greet(
         range_partners()
         + [("range", lax.rem(me + 1, ranges)), ("range", lax.rem(me + ranges - 1, ranges))]
         + [("pulse", lax.rem(z + shift, devices)) for shift in range(1, devices)]
     )
-    exchange(
-        samples_ref, taps_ref, taper_ref, cos_ref, sin_ref, table_ref, snapshot_ref,
-        low_ref, high_ref, padded_ref, outgoing_ref, gathered_ref, stage_ref, spread_ref, group,
-        sems[:6],
-    )
-    size = snapshot_ref.shape[1]
-    block = work_ref.shape[0]
-    for row in range(0, size, block):
-        gram = lax.dot_general(
-            snapshot_ref[:, row : row + block], snapshot_ref[:, : row + block],
-            (((0,), (0,)), ((), ())), precision=HIGHEST, preferred_element_type=jnp.float32,
-        )
-        for b_row, b_col, at in lower_blocks(size, block):
-            if b_row == row:
-                part_ref[at : at + block, :] = gram[:, b_col : b_col + block]
+    piece = gates // CHUNKS
+
+    def add_gram(part, first):
+        rows = slice(part * piece, (part + 1) * piece)
+        for row in range(0, size, block):
+            gram = lax.dot_general(
+                snapshot_ref[rows, row : row + block], snapshot_ref[rows, : row + block],
+                (((0,), (0,)), ((), ())), precision=HIGHEST, preferred_element_type=jnp.float32,
+            )
+            for b_row, b_col, at in lower_blocks(size, block):
+                if b_row == row:
+                    value = gram[:, b_col : b_col + block]
+                    if not first:
+                        value = part_ref[at : at + block, :] + value
+                    part_ref[at : at + block, :] = value
+
+    sent = exchange(
+        samples_ref, taps_ref, taper_ref, load, load_const, const_ref, snapshot_ref, low_ref,
+        high_ref, padded_ref, outgoing_ref, gathered_ref, stage_ref, spread_ref, group, sems[:6],
+        add_gram,
+    )
     sum_over_range(part_ref, pair_ref, half_ref, inbox_ref, total_ref, sems[6:])
-    out_ref[...] = snapshot_ref[...]
-    factor_and_solve(total_gates, total_ref, out_ref, cov_ref, work_ref)
+    written = []
+    count = piece // devices
+
+    def emit(column, part):
+        cols = slice(column * block, (column + 1) * block)
+        for source in range(devices):
+            at = part * piece + source * count
+            to = source * CHUNKS * count + part * count
+            copy = pltpu.make_async_copy(
+                snapshot_ref.at[at : at + count, cols], out_ref.at[to : to + count, cols],
+                out_sem.at[column, part, source],
+            )
+            copy.start()
+            written.append(copy)
+
+    factor_and_solve(
+        total_gates, total_ref, snapshot_ref, cov_ref, work_ref, inverse_ref, panel_ref, emit
+    )
+    for copy in sent:
+        copy.wait_send()
+    for copy in written:
+        copy.wait()
 
 
 def whiten_scratch(size, block, groups):
@@ -389,9 +456,7 @@
     count = share // CHUNKS
     block = min(BLOCK, width)
     cosine, sine, table = doppler_constants(bins * devices, devices, group)
-    room = -(-(tap_count + count) // LANES) * LANES
-    padded_taps = jnp.pad(taps, (0, room - tap_count))[None, :]
-    taper_row = jnp.repeat(taper, group)[None, :]
+    given = np.concatenate([table, cosine, sine], axis=0)
     buffers, sems = whiten_scratch(width, block, ranges // 2)
     dma = pltpu.SemaphoreType.DMA
     own = [
@@ -403,19 +468,27 @@
         pltpu.VMEM((devices, share, width), jnp.float32),
         pltpu.VMEM((devices * count, width), jnp.float32),
         pltpu.VMEM((devices, share, width), jnp.float32),
-    ]
-    pulse_sems = [dma((2,)), dma((2,))] + [dma((devices - 1, CHUNKS))] * 4
+        pltpu.VMEM(given.shape, jnp.float32),
+        pltpu.VMEM((block, block), jnp.float32),
+        pltpu.VMEM((width, block), jnp.float32),
+    ]
+    pulse_sems = [dma, dma, dma((width // block, CHUNKS, devices)), dma((2,)), dma((2,))] + [dma((devices - 1, CHUNKS))] * 4
     return pl.pallas_call(
         functools.partial(whole_kernel, gates * ranges, group),
         out_shape=jax.ShapeDtypeStruct(samples.shape, jnp.float32),
-        in_specs=[pl.BlockSpec(memory_space=pltpu.VMEM)] * 6,
-        out_specs=pl.BlockSpec(memory_space=pltpu.VMEM),
+        in_specs=[
+            pl.BlockSpec(memory_space=pl.ANY),
+            pl.BlockSpec(memory_space=pltpu.VMEM),
+            pl.BlockSpec(memory_space=pltpu.SMEM),
+            pl.BlockSpec(memory_space=pl.ANY),
+        ],
+        out_specs=pl.BlockSpec(memory_space=pl.ANY),
         scratch_shapes=own + buffers + pulse_sems + sems,
         compiler_params=pltpu.CompilerParams(
-            vmem_limit_bytes=48 << 20, collective_id=1, has_side_effects=True
+            vmem_limit_bytes=60 << 20, collective_id=1, has_side_effects=True
         ),
         name="whiten",
-    )(samples, padded_taps, taper_row, cosine, sine, table)
+    )(samples, taps[None, :], taper, given)
 
 
 def solution(mesh):

time: 143 us -> 132 us (0.923)
  Pallas kernels: 135 us -> 128 us
  local copies, waits for them, and re-layouts: 6.99 us -> 3.08 us
    pallas_call x1, Pallas kernels: 135 us -> 128 us  [local(): pl.pallas_call(functools.partial(whole_kernel, gates * ranges, group), ou...]
    unnamed x9 -> x1, local copies, waits for them, and re-layouts: 5.53 us -> 3.08 us
where the time goes in v4:
time: 132 us; the launch traced here: 131 us
  Pallas kernels  128 us (97%)
  local copies, waits for them, and re-layouts  3.08 us (2%)
    pallas_call x1, Pallas kernels, local(): pl.pallas_call(functools.partial(whole_kernel, gates * ranges, group), ou...  128 us
    unnamed x1, local copies, waits for them, and re-layouts  3.08 us

profile of v4, /device:TPU:0, one launch (start us, length us, event | category | flops | bytes accessed | tf_op | source)
XLA Modules:
  0.0 131.4 jit_solution(13287008979777882930)
XLA Ops:
  0.0 128.3 %whiten.1 = f32[1024,512]{1,0:T(8,128)} custom-call(f32[1024,512]{1,0:T(8,128)} %samples_ref.1, f32[1,128]{1,0:T(1,128)} %bitcast.1, f32[16]{0:T(128)} %taper_ref.1, f32[520,512]{1,0:T(8,128)} %constant.2.clone.given_ref), custom_call_target="tpu_custom_call" | custom-call | tf_op jit(solution)/shard_map/whiten/pallas_call | solution.py:476
  128.3 3.1 %copy.6 = f32[1024,512]{1,0:T(8,128)} copy(f32[1024,512]{1,0:T(8,128)} %whiten.1) | data formatting | bytes 4194304
